TPU v7x, 32 devices: a whole 2x2x4 slice. The times are simulated.
32 devices in a mesh: inst: 4 (over z), sector: 4 (over y, core), slab: 2 (over x).
Axes of the slice: x: 2, y: 2, z: 4, core: 2. Of those that a mesh axis runs over, the one named last changes fastest.
Arguments:
- adjoint_state: float32 [4, 4, 64, 8192], P('inst', None, None, ('sector', 'slab')), may hold values from -6 to 6
- mean_flow: float32 [3, 8192], P(None, ('sector', 'slab')), may hold values from -0.5 to 0.5
- metric: float32 [3, 8192], P(None, ('sector', 'slab')), may hold values from 0.5 to 2
- connectivity: int32 [6, 8192], P(None, ('sector', 'slab')), may hold values from 0 to 1279, as said below
- wall_flags: int32 [6, 8192], P(None, ('sector', 'slab')), may hold values 0 or 1
- donor_face_positions: int32 [4, 2048], P('inst', ('sector', 'slab')), may hold values from 0 to 510, as said below
- interp_weight: float32 [4], P('inst'), may hold values from 0 to 1
Outputs:
- residual: float32 [4, 4, 64, 8192], P('inst', None, None, ('sector', 'slab'))
- new_state: float32 [4, 4, 64, 8192], P('inst', None, None, ('sector', 'slab'))
Inputs may be any that keep to these rules, and one draw needn't show every extreme that they name: `connectivity`: within each block of 1024 columns: faces 0 to 3, face 4 of elements 256 and above and face 5 of elements below 768 name a local element below 1024; face 4 of the first 256 elements and face 5 of the last 256 elements name 1024 plus a distinct row of the neighbouring slab's layer. `donor_face_positions`: in each block of 256 columns, entry i of row t is i plus a rotation of instance t that is the same in every block.
All inputs are finite; a program needn't handle non-finite values. No bound on the sum of `wall_flags` on one device may be relied on, other than what follows from the above.
Results may differ from a plain program's by a relative error of at most 0.0003.
Values sent between devices are 32-bit elements; how exact they have to be, the bound alone decides.
No kernel may reach another device: no remote copies, remote signals or barrier semaphores. Data moves between devices by JAX's collectives and lax.ppermute only.
A program may use at most 192 MiB of HBM per device.

v0:
```python
import math
import jax
import jax.numpy as jnp
import numpy as np
from jax import lax
from jax.sharding import PartitionSpec as P

omega_scale = 0.5
nyquist_damping = 0.5
wave_bound = 1.5
pseudo_step = 0.05
maximum_harmonic = lax.Precision.HIGHEST


def padded_2(value, sides, width):
    for axis, dim in sides:
        size, length = (lax.axis_size(axis), value.shape[dim])
        up = [(i, (i + 1) % size) for i in range(size - 1)]
        down = [(j, i) for i, j in up]
        last = lax.slice_in_dim(value, length - width, length, axis=dim)
        leading = lax.slice_in_dim(value, 0, width, axis=dim)
        before = lax.ppermute(last, axis, up)
        after = lax.ppermute(leading, axis, down)
        value = jnp.concatenate([before, value, after], axis=dim)
    return value


def passed_along(value, axis, by):
    length = lax.axis_size(axis)
    return lax.ppermute(value, axis, [(i, (i + by) % length) for i in range(length)])


def derivative_tables():
    points = np.array([-1.0, -1.0 / math.sqrt(5.0), 1.0 / math.sqrt(5.0), 1.0])
    weights = np.array(
        [1.0 / np.prod([points[i] - points[m] for m in range(4) if m != i]) for i in range(4)]
    )
    matrix = np.zeros((4, 4))
    for i in range(4):
        for j in range(4):
            if i != j:
                matrix[i, j] = weights[j] / weights[i] / (points[i] - points[j])
        matrix[i, i] = -np.sum(matrix[i])
    identity = np.eye(4)
    return np.stack(
        [
            np.kron(np.kron(matrix, identity), identity),
            np.kron(np.kron(identity, matrix), identity),
            np.kron(np.kron(identity, identity), matrix),
        ]
    )


def selection_table():
    selector_matrix = np.zeros((96, 64))
    for f in range(6):
        k = f // 2
        layer_pos = 0 if f % 2 == 0 else 3
        for first in range(4):
            for second in range(4):
                indices = [first, second]
                indices.insert(k, layer_pos)
                selector_matrix[
                    16 * f + 4 * first + second, 16 * indices[0] + 4 * indices[1] + indices[2]
                ] = 1.0
    return selector_matrix


def spectral_matrix(count):
    row_index = jnp.arange(count, dtype=jnp.int32)[:, None]
    col_index = jnp.arange(count, dtype=jnp.int32)[None, :]
    offset = row_index - col_index
    parity = (1 - 2 * (offset % 2)).astype(jnp.float32)
    phase_angle = math.pi / count * offset.astype(jnp.float32)
    off_diag = offset != 0
    sine_val = jnp.where(off_diag, jnp.sin(phase_angle), 1.0)
    time_deriv = jnp.where(off_diag, 0.5 * parity * jnp.cos(phase_angle) / sine_val, 0.0)
    return -omega_scale * time_deriv - nyquist_damping / count * parity


def lookup_columns(lookup_table, columns):
    length = lookup_table.shape[2]
    indicator_matrix = (jnp.arange(length, dtype=jnp.int32)[:, None] == columns[None, :]).astype(
        jnp.float32
    )
    return jnp.einsum("xiz,zy->xiy", lookup_table, indicator_matrix, precision=maximum_harmonic)


def body_residual(
    state_of_block,
    spectral_term,
    differentiation_tables,
    selector_matrix,
    traces,
    mean_flow,
    metric,
    connectivity,
    wall_flags,
    ghost_low,
    ghost_high,
    iface_next,
    donor_positions,
    weight_value,
):
    variables = state_of_block.shape[0]
    elements = state_of_block.shape[2]
    iface_count = iface_next.shape[2]
    pseudo_gradient = (
        jnp.einsum(
            "fga,cat->fcgt", differentiation_tables, state_of_block, precision=maximum_harmonic
        )
        * metric[:, None, None, :]
    )
    advection = jnp.sum(mean_flow[:, None, None, :] * pseudo_gradient, axis=0)
    coupling = jnp.stack(
        [
            pseudo_gradient[0, 1] + pseudo_gradient[1, 2] + pseudo_gradient[2, 3],
            pseudo_gradient[0, 0],
            pseudo_gradient[1, 0],
            pseudo_gradient[2, 0],
        ]
    )
    residual = advection + coupling + spectral_term
    tables = [
        traces[0],
        traces[1],
        traces[2],
        traces[3],
        jnp.concatenate([traces[4], ghost_high], axis=2),
        jnp.concatenate([traces[5], ghost_low], axis=2),
    ]
    lifted_faces = []
    for f in range(6):
        k = f // 2
        orient = -1.0 if f % 2 == 0 else 1.0
        own_trace = traces[f]
        neighbour = lookup_columns(tables[f ^ 1], connectivity[f])
        mirror_sign = jnp.ones((variables,), jnp.float32).at[1 + k].set(-1.0)
        mirrored = own_trace * mirror_sign[:, None, None]
        neighbour = jnp.where(wall_flags[f][None, None, :] == 1, mirrored, neighbour)
        if f == 1:
            interface_rows = jnp.concatenate(
                [own_trace[:, :, elements - iface_count :], iface_next], axis=2
            )
            row_ids = jnp.arange(2 * iface_count, dtype=jnp.int32)[:, None]
            mixing_weight_matrix = (1.0 - weight_value) * (
                row_ids == donor_positions[None, :]
            ).astype(jnp.float32) + weight_value * (row_ids == donor_positions[None, :] + 1).astype(
                jnp.float32
            )
            blended = jnp.einsum(
                "xiz,zy->xiy", interface_rows, mixing_weight_matrix, precision=maximum_harmonic
            )
            neighbour = jnp.concatenate(
                [neighbour[:, :, : elements - iface_count], blended], axis=2
            )
        face_jump = neighbour - own_trace
        flux_jump = orient * mean_flow[k][None, None, :] * face_jump
        zero_row = jnp.zeros_like(face_jump[0])
        cross_terms = []
        for v in range(4):
            if v == 0:
                cross_terms.append(orient * face_jump[1 + k])
            elif v == 1 + k:
                cross_terms.append(orient * face_jump[0])
            else:
                cross_terms.append(zero_row)
        flux_jump = flux_jump + jnp.stack(cross_terms)
        lifted_faces.append(3.0 * metric[k][None, None, :] * (flux_jump + wave_bound * face_jump))
    lifted_everything = jnp.concatenate(lifted_faces, axis=1)
    return residual + jnp.einsum(
        "bc,sbh->sch", selector_matrix, lifted_everything, precision=maximum_harmonic
    )


def per_device(
    adjoint_state, mean_flow, metric, connectivity, wall_flags, donor_face_positions, interp_weight
):
    state_of_block = adjoint_state[0]
    variables, node_count, elements = state_of_block.shape
    rim_width = elements // 4
    iface_count = donor_face_positions.shape[1]
    differentiation_tables = jnp.asarray(derivative_tables(), jnp.float32)
    selector_matrix = jnp.asarray(selection_table(), jnp.float32)
    every_trace_set = jnp.einsum(
        "qa,yas->yqs", selector_matrix, state_of_block, precision=maximum_harmonic
    )
    traces = [every_trace_set[:, 16 * f : 16 * f + 16, :] for f in range(6)]
    slab_edge_rows = jnp.concatenate(
        [traces[4][:, :, :rim_width], traces[5][:, :, elements - rim_width :]], axis=2
    )
    padded = padded_2(slab_edge_rows, (("slab", 2),), rim_width)
    ghost_low = padded[:, :, :rim_width]
    ghost_high = padded[:, :, 3 * rim_width :]
    iface_next = passed_along(traces[1][:, :, elements - iface_count :], "sector", -1)
    spectral = spectral_matrix(lax.axis_size("inst"))
    flat_state = state_of_block.reshape(1, variables, node_count * elements)
    inst_row = lax.dynamic_index_in_dim(spectral, lax.axis_index("inst"), 0, keepdims=False)
    spectral_flat = jnp.einsum(
        "j,jvc->vc",
        inst_row,
        lax.all_gather(flat_state, "inst", axis=0, tiled=True),
        precision=maximum_harmonic,
    )
    spectral_term = spectral_flat.reshape(variables, node_count, elements)
    residual = body_residual(
        state_of_block,
        spectral_term,
        differentiation_tables,
        selector_matrix,
        traces,
        mean_flow,
        metric,
        connectivity,
        wall_flags,
        ghost_low,
        ghost_high,
        iface_next,
        donor_face_positions[0],
        interp_weight[0],
    )
    return (residual[None], (state_of_block + pseudo_step * residual)[None])


def solution(mesh):
    return jax.shard_map(
        per_device,
        mesh=mesh,
        in_specs=(
            P("inst", None, None, ("sector", "slab")),
            P(None, ("sector", "slab")),
            P(None, ("sector", "slab")),
            P(None, ("sector", "slab")),
            P(None, ("sector", "slab")),
            P("inst", ("sector", "slab")),
            P("inst"),
        ),
        out_specs=(
            P("inst", None, None, ("sector", "slab")),
            P("inst", None, None, ("sector", "slab")),
        ),
        check_vma=False,
    )
```

profile of v0, /device:TPU:0, one launch (start us, length us, event | category | flops | bytes accessed | tf_op | source)
XLA Modules:
  0.0 124.0 jit_solution(17806464936114319551)
XLA Ops:
  7.2 0.0 all-gather.2.cloned.1.call-start
  7.2 3.0 %reshape_squeeze.3 = f32[1,4,65536]{2,1,0:T(4,128)} reshape(f32[1,4,64,1024]{3,2,1,0:T(8,128)} %param.21) | data formatting | bytes 2097152 | tf_op jit(solution)/shard_map/reshape;squeeze | solution.py:197
  10.2 0.0 all-gather.2.cloned.1.call-update
  10.3 0.0 copy-start.13
  10.3 1.4 %convolution_bitcast_fusion = f32[4,96,1024]{2,1,0:T(8,128)S(1)} fusion(f32[96,64,1]{0,1,2:T(8,128)S(1)} %copy-done.4, f32[1,4,64,1024]{3,2,1,0:T(8,128)S(1)} %copy-done), kind=kOutput, calls=%fused_computation.28 | convolution fusion | flops 301989888 | bytes 2646016 | tf_op jit(solution)/shard_map/qa,yas->yqs/dot_general | solution.py:185
  11.8 0.7 fusion.126
  12.4 1.3 %collective-permute-start.2 = (f32[4,16,256]{2,1,0:T(8,128)S(1)}, f32[4,16,256]{2,1,0:T(8,128)}, u32[]{:S(2)}, u32[]{:S(2)}) collective-permute-start(f32[4,16,256]{2,1,0:T(8,128)S(1)} %get-tuple-element.75), channel_id=1, source_target_pairs={{1,0},{3,2},{5,4},{7,6},{9,8},{11,10},{13,12},{15,14},{17,16},{19,... | collective-permute-start | bytes 196616 | tf_op jit(solution)/shard_map/ppermute | solution.py:23
  13.7 6.1 %collective-permute-start.1 = (f32[4,16,256]{2,1,0:T(8,128)}, f32[4,16,256]{2,1,0:T(8,128)}, u32[]{:S(2)}, u32[]{:S(2)}) collective-permute-start(f32[4,16,256]{2,1,0:T(8,128)} %get-tuple-element.76), channel_id=1, source_target_pairs={{0,1},{2,3},{4,5},{6,7},{8,9},{10,11},{12,13},{14,15},{16,17},{18,... | collective-permute-start | bytes 196616 | tf_op jit(solution)/shard_map/ppermute | solution.py:22
  19.8 1.5 %collective-permute-start = (f32[4,16,256]{2,1,0:T(8,128)}, f32[4,16,256]{2,1,0:T(8,128)}, u32[]{:S(2)}, u32[]{:S(2)}) collective-permute-start(f32[4,16,256]{2,1,0:T(8,128)} %get-tuple-element.77), channel_id=1, source_target_pairs={{0,6},{2,0},{4,2},{6,4},{1,7},{3,1},{5,3},{7,5},{8,14},{10,8},{12,... | collective-permute-start | bytes 196616 | tf_op jit(solution)/shard_map/ppermute | solution.py:30
  22.1 0.1 compare_reduce_fusion
  22.3 1.7 %fusion.36 = f32[4,16,1024]{2,1,0:T(8,128)S(1)} fusion(s32[1024]{0:T(1024)S(1)} %bitcast.131, f32[4,96,1024]{2,1,0:T(8,128)S(1)} %convolution_bitcast_fusion, f32[4]{0:T(128)S(1)} %copy-done.13, pred[1024]{0:T(1024)(128)(4,1)S(1)} %get-tuple-element.64), kind=kOutput, calls=%fused_computation.34 | convolution fusion | flops 806551552 | bytes 792064 | tf_op jit(solution)/shard_map/xiz,zy->xiy/dot_general | solution.py:86
  24.0 1.7 %fusion.42 = f32[4,16,1024]{2,1,0:T(8,128)S(1)} fusion(s32[1024]{0:T(1024)S(1)} %bitcast.130, f32[4,96,1024]{2,1,0:T(8,128)S(1)} %convolution_bitcast_fusion, f32[4]{0:T(128)S(1)} %copy-done.13, pred[1024]{0:T(1024)(128)(4,1)S(1)} %get-tuple-element.63), kind=kOutput, calls=%fused_computation.36 | convolution fusion | flops 806551552 | bytes 792064 | tf_op jit(solution)/shard_map/xiz,zy->xiy/dot_general | solution.py:86
  25.7 1.6 %fusion.30 = f32[4,16,1024]{2,1,0:T(8,128)S(1)} fusion(s32[1024]{0:T(1024)S(1)} %bitcast.129, f32[4,96,1024]{2,1,0:T(8,128)S(1)} %convolution_bitcast_fusion, f32[4]{0:T(128)S(1)} %copy-done.11, pred[1024]{0:T(1024)(128)(4,1)S(1)} %get-tuple-element.66), kind=kOutput, calls=%fused_computation.32 | convolution fusion | flops 806551552 | bytes 792064 | tf_op jit(solution)/shard_map/xiz,zy->xiy/dot_general | solution.py:86
  27.4 1.6 %fusion.16 = f32[4,16,1024]{2,1,0:T(8,128)S(1)} fusion(s32[1024]{0:T(1024)S(1)} %bitcast.128, f32[4,96,1024]{2,1,0:T(8,128)S(1)} %convolution_bitcast_fusion), kind=kOutput, calls=%fused_computation.18 | convolution fusion | flops 806354944 | bytes 528384 | tf_op jit(solution)/shard_map/xiz,zy->xiy/dot_general | solution.py:86
  29.0 0.8 fusion.95
  29.8 0.1 slice_select_fusion
  29.9 3.7 %multiply_reduce_fusion = (f32[4,64,1024]{2,1,0:T(8,128)}, f32[3,4,64,1024]{3,2,1,0:T(8,128)S(1)}) fusion(f32[3,1024]{1,0:T(4,128)S(1)} %copy-done.6, f32[3,1024]{1,0:T(4,128)S(1)} %copy-done.7, f32[3,64,64,1]{2,1,3,0:T(8,128)S(1)} %copy-done.5, f32[1,4,64,1024]{3,2,1,0:T(8,128)S(1)} %copy-done), kind=kOutput, calls=%fused_computation.21 | convolution fusion | flops 606076928 | bytes 5316608 | tf_op jit(solution)/shard_map/fga,cat->fcgt/dot_general | solution.py:109
  33.6 0.8 fusion.100
  34.5 1.4 %fusion.61 = f32[4,16,256]{2,1,0:T(8,128)S(1)} fusion(f32[]{:T(128)} %bitcast.110, s32[256]{0:T(256)S(1)} %bitcast.133, f32[]{:T(128)S(6)} %sub.46, s32[256]{0:T(256)S(1)} %bitcast.132, f32[4,16,256]{2,1,0:T(8,128)} %collective-permute-done, f32[4,16,256]{2,1,0:T(8,128)} %get-tuple-element.77), kind=kOutput, calls=%fused_computation.47 | convolution fusion | flops 101351424 | bytes 198664 | tf_op jit(solution)/shard_map/xiz,zy->xiy/dot_general | solution.py:151
  35.9 0.1 fusion.125
  36.0 2.9 %fusion.48 = f32[4,16,1024]{2,1,0:T(8,128)S(1)} fusion(s32[1024]{0:T(1024)S(1)} %bitcast.127, f32[4,16,256]{2,1,0:T(8,128)} %collective-permute-done.1, f32[4,16,1024]{2,1,0:T(8,128)S(1)} %get-tuple-element.74, f32[4]{0:T(128)S(1)} %copy-done.12, pred[1024]{0:T(1024)(128)(4,1)S(1)} %get-tuple-element.67, f32[4,96,1024]{2,1,0:T(8,128)S(1)} %convolution_bitcast_fusion), kind=kOutput, calls=%fused_computation.38 | convolution fusion | flops 1008222208 | bytes 857104 | tf_op jit(solution)/shard_map/xiz,zy->xiy/dot_general | solution.py:86
  38.9 3.1 %fusion.54 = f32[4,16,1024]{2,1,0:T(8,128)S(1)} fusion(s32[1024]{0:T(1024)S(1)} %bitcast.126, f32[4,16,256]{2,1,0:T(8,128)} %collective-permute-done.2, f32[4,16,1024]{2,1,0:T(8,128)S(1)} %get-tuple-element.72, f32[4]{0:T(128)S(1)} %copy-done.12, pred[1024]{0:T(1024)(128)(4,1)S(1)} %get-tuple-element.62, f32[4,96,1024]{2,1,0:T(8,128)S(1)} %convolution_bitcast_fusion), kind=kOutput, calls=%fused_computation.40 | convolution fusion | flops 1008222208 | bytes 857104 | tf_op jit(solution)/shard_map/xiz,zy->xiy/dot_general | solution.py:86
  42.0 0.8 fusion.99
  42.8 0.8 fusion.87
  43.5 0.8 fusion.91
  44.3 0.7 fusion.76
  45.0 0.8 fusion.81
  45.8 48.1 %all-gather.2.cloned.1.call-done = f32[4,4,65536]{2,1,0:T(4,128)} async-done(((f32[1,4,65536]{2,1,0:T(4,128)}), f32[4,4,65536]{2,1,0:T(4,128)}) %all-gather.2.cloned.1.call-update) | async-done | bytes 4194320 | tf_op jit(solution)/shard_map/all_gather | solution.py:202
  93.9 6.1 %dot_general.39 = f32[4,64,1024,4]{2,1,0,3:T(8,128)} reshape(f32[4,65536,4]{1,0,2:T(4,128)} %bitcast.111) | data formatting | bytes 8388608 | tf_op jit(solution)/shard_map/j,jvc->vc/dot_general | solution.py:199
  100.0 12.7 %fusion.6 = f32[1,4,64,1024]{3,0,2,1:T(1,128)S(1)} fusion(f32[4,64,1024,4]{2,1,0,3:T(8,128)} %dot_general.39, f32[4,4]{1,0:T(4,128)S(1)} %multiply_subtract_fusion, s32[]{:T(128)S(6)} %select_n.40), kind=kOutput, calls=%fused_computation.6 | convolution fusion | flops 12582912 | bytes 5243396 | tf_op jit(solution)/shard_map/j,jvc->vc/dot_general | solution.py:199
  112.7 3.1 %fusion.26 = f32[4,64,1024]{2,1,0:T(8,128)S(1)} fusion(f32[4,96,1024]{2,1,0:T(8,128)} %fusion.81, f32[96,64,1]{0,1,2:T(8,128)S(1)} %copy-done.4, f32[4,64,1024]{2,1,0:T(8,128)S(1)} %copy-done.2, f32[1,64,1024]{2,1,0:T(8,128)S(1)} %get-tuple-element.70, f32[1,64,1024]{2,1,0:T(8,128)S(1)} %copy-done.3, f32[1,64,1024]{2,1,0:T(8,128)S(1)} %get-tuple-element.69, ...), kind=kOutput, calls=%fused_computation.30 | convolution fusion | flops 303562752 | bytes 5791744 | tf_op jit(solution)/shard_map/bc,sbh->sch/dot_general | solution.py:171
  115.8 1.3 %fusion.60 = f32[1,4,64,1024]{3,2,1,0:T(8,128)} fusion(f32[1,4,64,1024]{3,2,1,0:T(8,128)S(1)} %copy-done, f32[4,64,1024]{2,1,0:T(8,128)S(1)} %fusion.26), kind=kLoop, calls=%fused_computation.46 | loop fusion | flops 524288 | bytes 3145728 | tf_op jit(solution)/shard_map/broadcast_in_dim | solution.py:222
  (47 shorter events, 0.3 us)
Async XLA Ops:
  7.2 3.1 %copy-start.4 = (f32[96,64,1]{0,1,2:T(8,128)S(1)}, f32[96,64,1]{0,1,2:T(8,128)}, u32[]{:S(2)}) copy-start(f32[96,64,1]{0,1,2:T(8,128)} %constant.191) | copy-start | bytes 73732
  7.2 3.1 %copy-start = (f32[1,4,64,1024]{3,2,1,0:T(8,128)S(1)}, f32[1,4,64,1024]{3,2,1,0:T(8,128)}, u32[]{:S(2)}) copy-start(f32[1,4,64,1024]{3,2,1,0:T(8,128)} %param.21) | copy-start | bytes 3145732
  7.2 86.7 %all-gather.2.cloned.1.call-start = ((), (), s32[]{:S(2)}) async-start(), calls=%async_computation | async-start | bytes 5242880 | tf_op jit(solution)/shard_map/all_gather | solution.py:202
  10.3 11.8 %copy-start.9 = (s32[6,1024]{1,0:T(8,128)S(1)}, s32[6,1024]{1,0:T(8,128)}, u32[]{:S(2)}) copy-start(s32[6,1024]{1,0:T(8,128)} %param.25) | copy-start | bytes 73732
  10.3 11.9 %copy-start.6 = (f32[3,1024]{1,0:T(4,128)S(1)}, f32[3,1024]{1,0:T(4,128)}, u32[]{:S(2)}) copy-start(f32[3,1024]{1,0:T(4,128)} %param.22) | copy-start | bytes 36868
  10.3 11.9 %copy-start.10 = (s32[1,256]{1,0:T(1,128)S(1)}, s32[1,256]{1,0:T(1,128)}, u32[]{:S(2)}) copy-start(s32[1,256]{1,0:T(1,128)} %param.26) | copy-start | bytes 3076
  10.3 11.9 %copy-start.7 = (f32[3,1024]{1,0:T(4,128)S(1)}, f32[3,1024]{1,0:T(4,128)}, u32[]{:S(2)}) copy-start(f32[3,1024]{1,0:T(4,128)} %param.23) | copy-start | bytes 36868
  10.3 11.9 %copy-start.8 = (s32[6,1024]{1,0:T(8,128)S(1)}, s32[6,1024]{1,0:T(8,128)}, u32[]{:S(2)}) copy-start(s32[6,1024]{1,0:T(8,128)} %param.24) | copy-start | bytes 73732
  10.3 12.0 %copy-start.13 = (f32[4]{0:T(128)S(1)}, f32[4]{0:T(128)}, u32[]{:S(2)}) copy-start(f32[4]{0:T(128)} %constant.182.clone.1) | copy-start | bytes 52
  12.4 26.4 %collective-permute-start.2 = (f32[4,16,256]{2,1,0:T(8,128)S(1)}, f32[4,16,256]{2,1,0:T(8,128)}, u32[]{:S(2)}, u32[]{:S(2)}) collective-permute-start(f32[4,16,256]{2,1,0:T(8,128)S(1)} %get-tuple-element.75), channel_id=1, source_target_pairs={{1,0},{3,2},{5,4},{7,6},{9,8},{11,10},{13,12},{15,14},{17,16},{19,... | collective-permute-start | bytes 196616 | tf_op jit(solution)/shard_map/ppermute | solution.py:23
  13.7 22.2 %collective-permute-start.1 = (f32[4,16,256]{2,1,0:T(8,128)}, f32[4,16,256]{2,1,0:T(8,128)}, u32[]{:S(2)}, u32[]{:S(2)}) collective-permute-start(f32[4,16,256]{2,1,0:T(8,128)} %get-tuple-element.76), channel_id=1, source_target_pairs={{0,1},{2,3},{4,5},{6,7},{8,9},{10,11},{12,13},{14,15},{16,17},{18,... | collective-permute-start | bytes 196616 | tf_op jit(solution)/shard_map/ppermute | solution.py:22
  19.8 14.7 %collective-permute-start = (f32[4,16,256]{2,1,0:T(8,128)}, f32[4,16,256]{2,1,0:T(8,128)}, u32[]{:S(2)}, u32[]{:S(2)}) collective-permute-start(f32[4,16,256]{2,1,0:T(8,128)} %get-tuple-element.77), channel_id=1, source_target_pairs={{0,6},{2,0},{4,2},{6,4},{1,7},{3,1},{5,3},{7,5},{8,14},{10,8},{12,... | collective-permute-start | bytes 196616 | tf_op jit(solution)/shard_map/ppermute | solution.py:30
  24.0 1.7 %copy-start.11 = (f32[4]{0:T(128)S(1)}, f32[4]{0:T(128)}, u32[]{:S(2)}) copy-start(f32[4]{0:T(128)} %constant.180.clone.1) | copy-start | bytes 52
  27.4 2.5 %copy-start.5 = (f32[3,64,64,1]{2,1,3,0:T(8,128)S(1)}, f32[3,64,64,1]{2,1,3,0:T(8,128)}, u32[]{:S(2)}) copy-start(f32[3,64,64,1]{2,1,3,0:T(8,128)} %constant.190) | copy-start | bytes 147460
  34.4 1.5 %copy-start.12 = (f32[4]{0:T(128)S(1)}, f32[4]{0:T(128)}, u32[]{:S(2)}) copy-start(f32[4]{0:T(128)} %constant.183.clone.1) | copy-start | bytes 52
  99.9 12.8 %copy-start.2 = (f32[4,64,1024]{2,1,0:T(8,128)S(1)}, f32[4,64,1024]{2,1,0:T(8,128)}, u32[]{:S(2)}) copy-start(f32[4,64,1024]{2,1,0:T(8,128)} %get-tuple-element.102) | copy-start | bytes 3145732
  99.9 12.8 %copy-start.3 = (f32[1,64,1024]{2,1,0:T(8,128)S(1)}, f32[1,64,1024]{2,1,0:T(8,128)}, u32[]{:S(2)}) copy-start(f32[1,64,1024]{2,1,0:T(8,128)} %get-tuple-element.71) | copy-start | bytes 786436
  115.8 1.3 %copy-start.1 = (f32[4,64,1024]{2,1,0:T(8,128)}, f32[4,64,1024]{2,1,0:T(8,128)S(1)}, u32[]{:S(2)}) copy-start(f32[4,64,1024]{2,1,0:T(8,128)S(1)} %fusion.26) | copy-start | bytes 3145732
Sparse Core Ops, SparseCore 0:
  10.4 83.4 all-gather.1
where the time goes:
time: 124 us
  waiting for transfers between devices  48.1 us (39%)
  matrix products  34.9 us (28%)
  between operations  15.1 us (12%)
  local copies, waits for them, and re-layouts  9.9 us (8%)
  starting transfers between devices  8.95 us (7%)
  other arithmetic  7.01 us (6%)
    all_gather x1, waiting for transfers between devices, per_device(): lax.all_gather(flat_state, 'inst', axis=0, tiled=True)  48.1 us
    dot_general x1, matrix products, per_device(): jnp.einsum('j,jvc->vc', inst_row, lax.all_gather(flat_state, 'inst', axis...  12.7 us
    dot_general x6, matrix products, lookup_columns(): jnp.einsum('xiz,zy->xiy', lookup_table, indicator_matrix, precision=maxim...  12.5 us
    ppermute x1, starting transfers between devices, padded_2(): before = lax.ppermute(last, axis, up)  6.09 us
    dot_general x1, local copies, waits for them, and re-layouts, per_device(): jnp.einsum('j,jvc->vc', inst_row, lax.all_gather(flat_state, 'inst', axis...  6.08 us
    unnamed x5, other arithmetic  3.76 us
    dot_general x1, matrix products, body_residual(): jnp.einsum('fga,cat->fcgt', differentiation_tables, state_of_block, preci...  3.74 us
    dot_general x1, matrix products, body_residual(): jnp.einsum('bc,sbh->sch', selector_matrix, lifted_everything, precision=m...  3.09 us
  transfers between devices with their start and end apart: 4, of which 1 were waited for; matrix products, arithmetic and copies ran while one was open for 21% of the time, Pallas kernels for 0%

commit v1 on v0

--- a/solution.py
+++ b/solution.py
@@ -196,12 +196,38 @@
     spectral = spectral_matrix(lax.axis_size("inst"))
     flat_state = state_of_block.reshape(1, variables, node_count * elements)
     inst_row = lax.dynamic_index_in_dim(spectral, lax.axis_index("inst"), 0, keepdims=False)
-    spectral_flat = jnp.einsum(
+    size_2, here, extent = (lax.axis_size("inst"), lax.axis_index("inst"), flat_state.shape[0])
+    right = [(i_2, (i_2 + 1) % size_2) for i_2 in range(size_2)]
+    left = [(i_2, (i_2 - 1) % size_2) for i_2 in range(size_2)]
+    halfway = size_2 // 2
+    from_left = from_right = flat_state
+    so_far = jnp.einsum(
         "j,jvc->vc",
-        inst_row,
-        lax.all_gather(flat_state, "inst", axis=0, tiled=True),
+        lax.dynamic_slice_in_dim(inst_row, here * extent, flat_state.shape[0], axis=0),
+        flat_state,
         precision=maximum_harmonic,
     )
+    for step in range(1, halfway + 1):
+        from_left = lax.ppermute(from_left, "inst", right)
+        if step < size_2 - halfway:
+            from_right = lax.ppermute(from_right, "inst", left)
+            so_far = so_far + jnp.einsum(
+                "j,jvc->vc",
+                lax.dynamic_slice_in_dim(
+                    inst_row, (here + step) % size_2 * extent, from_right.shape[0], axis=0
+                ),
+                from_right,
+                precision=maximum_harmonic,
+            )
+        so_far = so_far + jnp.einsum(
+            "j,jvc->vc",
+            lax.dynamic_slice_in_dim(
+                inst_row, (here - step) % size_2 * extent, from_left.shape[0], axis=0
+            ),
+            from_left,
+            precision=maximum_harmonic,
+        )
+    spectral_flat = so_far
     spectral_term = spectral_flat.reshape(variables, node_count, elements)
     residual = body_residual(
         state_of_block,

time: 124 us -> 84.8 us (0.68)
  waiting for transfers between devices: 48.1 us -> 28.2 us
  matrix products: 34.9 us -> 21 us
  between operations: 15.1 us -> 2.15 us
  other arithmetic: 7.01 us -> 12.7 us
  starting transfers between devices: 8.95 us -> 12.4 us
  local copies, waits for them, and re-layouts: 9.9 us -> 7.98 us
    all_gather x1 -> x0, waiting for transfers between devices: 48.1 us -> none  [per_device(): lax.all_gather(flat_state, 'inst', axis=0, tiled=True)]
    ppermute x0 -> x3, waiting for transfers between devices: none -> 28.1 us  [the longest x2 22.7 us: per_device(): from_left = lax.ppermute(from_left, 'inst', right)]
    dot_general x1 -> x0, matrix products: 12.7 us -> none  [per_device(): jnp.einsum('j,jvc->vc', inst_row, lax.all_gather(flat_state, 'inst', axis...]
    dot_general x1 -> x0, local copies, waits for them, and re-layouts: 6.08 us -> none  [per_device(): jnp.einsum('j,jvc->vc', inst_row, lax.all_gather(flat_state, 'inst', axis...]
    ppermute x0 -> x3, starting transfers between devices: none -> 5.26 us  [the longest x2 3.16 us: per_device(): from_left = lax.ppermute(from_left, 'inst', right)]
    add x0 -> x1, other arithmetic: none -> 3.95 us  [per_device(): so_far + jnp.einsum('j,jvc->vc', lax.dynamic_slice_in_dim(inst_row, (here...]
    unnamed x5 -> x6, other arithmetic: 3.76 us -> 1.69 us
    unnamed x28 -> x75, local copies, waits for them, and re-layouts: 0.08 us -> 2.15 us
  transfers between devices with their start and end apart: 4 -> 6, of which waited for: 1 -> 2; matrix products, arithmetic and copies ran while one was open for 21% -> 37% of each run, Pallas kernels for 0% -> 0%
where the time goes in v1:
time: 84.8 us; the launch traced here: 84.4 us
  waiting for transfers between devices  28.2 us (33%)
  matrix products  21 us (25%)
  other arithmetic  12.7 us (15%)
  starting transfers between devices  12.4 us (15%)
  local copies, waits for them, and re-layouts  7.98 us (9%)
  between operations  2.15 us (3%)
    ppermute x2, waiting for transfers between devices, per_device(): from_left = lax.ppermute(from_left, 'inst', right)  22.7 us
    dot_general x6, matrix products, lookup_columns(): jnp.einsum('xiz,zy->xiy', lookup_table, indicator_matrix, precision=maxim...  12.5 us
    ppermute x1, starting transfers between devices, padded_2(): before = lax.ppermute(last, axis, up)  5.77 us
    ppermute x1, waiting for transfers between devices, per_device(): from_right = lax.ppermute(from_right, 'inst', left)  5.41 us
    add x1, other arithmetic, per_device(): so_far + jnp.einsum('j,jvc->vc', lax.dynamic_slice_in_dim(inst_row, (here...  3.95 us
    dot_general x1, matrix products, body_residual(): jnp.einsum('fga,cat->fcgt', differentiation_tables, state_of_block, preci...  3.78 us
    ppermute x2, starting transfers between devices, per_device(): from_left = lax.ppermute(from_left, 'inst', right)  3.16 us
    another operation x1, local copies, waits for them, and re-layouts, per_device(): flat_state = state_of_block.reshape(1, variables, node_count * elements)  3 us
  transfers between devices with their start and end apart: 6, of which 2 were waited for; matrix products, arithmetic and copies ran while one was open for 37% of the time, Pallas kernels for 0%

profile of v1, /device:TPU:0, one launch (start us, length us, event | category | flops | bytes accessed | tf_op | source)
XLA Modules:
  0.0 84.4 jit_solution(9165420507817469701)
XLA Ops:
  0.7 3.0 %reshape_squeeze.3 = f32[1,4,65536]{2,1,0:T(4,128)} reshape(f32[1,4,64,1024]{3,2,1,0:T(8,128)} %param.21) | data formatting | bytes 2097152 | tf_op jit(solution)/shard_map/reshape;squeeze | solution.py:197
  3.7 3.1 %collective-permute-start.1 = (f32[1,4,65536]{2,1,0:T(4,128)}, f32[1,4,65536]{2,1,0:T(4,128)}, u32[]{:S(2)}, u32[]{:S(2)}) collective-permute-start(f32[1,4,65536]{2,1,0:T(4,128)} %reshape_squeeze.3), channel_id=1, source_target_pairs={{0,8},{8,16},{16,24},{24,0},{1,9},{9,17},{17,25},{25,1},{2,10},{10... | collective-permute-start | bytes 3145736 | tf_op jit(solution)/shard_map/ppermute | solution.py:211
  6.8 2.1 %collective-permute-start = (f32[1,4,65536]{2,1,0:T(4,128)}, f32[1,4,65536]{2,1,0:T(4,128)}, u32[]{:S(2)}, u32[]{:S(2)}) collective-permute-start(f32[1,4,65536]{2,1,0:T(4,128)} %reshape_squeeze.3), channel_id=1, source_target_pairs={{0,24},{8,0},{16,8},{24,16},{1,25},{9,1},{17,9},{25,17},{2,26},{10... | collective-permute-start | bytes 3145736 | tf_op jit(solution)/shard_map/ppermute | solution.py:213
  8.9 1.4 %convolution_bitcast_fusion = f32[4,96,1024]{2,1,0:T(8,128)S(1)} fusion(f32[96,64,1]{0,1,2:T(8,128)S(1)} %copy-done.16, f32[1,4,64,1024]{3,2,1,0:T(8,128)S(1)} %copy-done), kind=kOutput, calls=%fused_computation.26 | convolution fusion | flops 301989888 | bytes 2646016 | tf_op jit(solution)/shard_map/qa,yas->yqs/dot_general | solution.py:185
  10.3 0.7 fusion.120
  11.0 1.3 %collective-permute-start.5 = (f32[4,16,256]{2,1,0:T(8,128)}, f32[4,16,256]{2,1,0:T(8,128)}, u32[]{:S(2)}, u32[]{:S(2)}) collective-permute-start(f32[4,16,256]{2,1,0:T(8,128)} %get-tuple-element.75), channel_id=1, source_target_pairs={{1,0},{3,2},{5,4},{7,6},{9,8},{11,10},{13,12},{15,14},{17,16},{19,... | collective-permute-start | bytes 196616 | tf_op jit(solution)/shard_map/ppermute | solution.py:23
  12.3 5.8 %collective-permute-start.4 = (f32[4,16,256]{2,1,0:T(8,128)}, f32[4,16,256]{2,1,0:T(8,128)}, u32[]{:S(2)}, u32[]{:S(2)}) collective-permute-start(f32[4,16,256]{2,1,0:T(8,128)} %get-tuple-element.76), channel_id=1, source_target_pairs={{0,1},{2,3},{4,5},{6,7},{8,9},{10,11},{12,13},{14,15},{16,17},{18,... | collective-permute-start | bytes 196616 | tf_op jit(solution)/shard_map/ppermute | solution.py:22
  18.3 0.6 compare_reduce_fusion
  18.9 0.6 broadcast_multiply_fusion
  20.1 0.6 fusion.124
  20.8 0.7 fusion.126
  21.4 0.7 multiply_bitcast_fusion.1
  22.2 1.6 %fusion.34 = f32[4,16,1024]{2,1,0:T(8,128)S(1)} fusion(s32[1024]{0:T(1024)S(1)} %bitcast.143, f32[4,96,1024]{2,1,0:T(8,128)S(1)} %convolution_bitcast_fusion, f32[4]{0:T(128)S(1)} %copy-done.36, pred[1024]{0:T(1024)(128)(4,1)S(1)} %get-tuple-element.64), kind=kOutput, calls=%fused_computation.32 | convolution fusion | flops 806551552 | bytes 792064 | tf_op jit(solution)/shard_map/xiz,zy->xiy/dot_general | solution.py:86
  23.9 0.6 slice_multiply_fusion.4
  24.6 1.6 %fusion.40 = f32[4,16,1024]{2,1,0:T(8,128)S(1)} fusion(s32[1024]{0:T(1024)S(1)} %bitcast.142, f32[4,96,1024]{2,1,0:T(8,128)S(1)} %convolution_bitcast_fusion, f32[4]{0:T(128)S(1)} %copy-done.36, pred[1024]{0:T(1024)(128)(4,1)S(1)} %get-tuple-element.63), kind=kOutput, calls=%fused_computation.34 | convolution fusion | flops 806551552 | bytes 792064 | tf_op jit(solution)/shard_map/xiz,zy->xiy/dot_general | solution.py:86
  26.2 0.7 fusion.122
  26.9 1.7 %fusion.28 = f32[4,16,1024]{2,1,0:T(8,128)S(1)} fusion(s32[1024]{0:T(1024)S(1)} %bitcast.141, f32[4,96,1024]{2,1,0:T(8,128)S(1)} %convolution_bitcast_fusion, f32[4]{0:T(128)S(1)} %copy-done.34, pred[1024]{0:T(1024)(128)(4,1)S(1)} %get-tuple-element.66), kind=kOutput, calls=%fused_computation.30 | convolution fusion | flops 806551552 | bytes 792064 | tf_op jit(solution)/shard_map/xiz,zy->xiy/dot_general | solution.py:86
  28.6 1.6 %fusion.14 = f32[4,16,1024]{2,1,0:T(8,128)S(1)} fusion(s32[1024]{0:T(1024)S(1)} %bitcast.140, f32[4,96,1024]{2,1,0:T(8,128)S(1)} %convolution_bitcast_fusion), kind=kOutput, calls=%fused_computation.16 | convolution fusion | flops 806354944 | bytes 528384 | tf_op jit(solution)/shard_map/xiz,zy->xiy/dot_general | solution.py:86
  30.3 3.8 %multiply_reduce_fusion = (f32[4,64,1024]{2,1,0:T(8,128)}, f32[3,4,64,1024]{3,2,1,0:T(8,128)S(1)}) fusion(f32[3,1024]{1,0:T(4,128)S(1)} %copy-done.19, f32[3,1024]{1,0:T(4,128)S(1)} %copy-done.20, f32[3,64,64,1]{2,1,3,0:T(8,128)S(1)} %copy-done.18, f32[1,4,64,1024]{3,2,1,0:T(8,128)S(1)} %copy-done), kind=kOutput, calls=%fused_computation.19 | convolution fusion | flops 606076928 | bytes 5316608 | tf_op jit(solution)/shard_map/fga,cat->fcgt/dot_general | solution.py:109
  34.1 0.8 fusion.97
  35.0 0.8 slice_select_fusion
  35.8 0.8 fusion.92
  37.8 1.6 %copy.12 = f32[1,4,64,1024]{3,1,2,0:T(4,128)} copy(f32[1,4,64,1024]{3,2,1,0:T(8,128)S(1)} %multiply_bitcast_fusion.1) | data formatting | bytes 2097152
  39.4 1.4 %fusion.58 = f32[4,16,256]{2,1,0:T(8,128)S(1)} fusion(f32[]{:T(128)} %bitcast.121, s32[256]{0:T(256)} %bitcast.145, f32[]{:T(128)S(6)} %sub.84, s32[256]{0:T(256)} %bitcast.144, f32[4,16,256]{2,1,0:T(8,128)} %collective-permute-done.3, f32[4,16,256]{2,1,0:T(8,128)} %get-tuple-element.77), kind=kOutput, calls=%fused_computation.49 | convolution fusion | flops 101351424 | bytes 198664 | tf_op jit(solution)/shard_map/xiz,zy->xiy/dot_general | solution.py:151
  40.8 1.0 %fusion.119 = (f32[4,16,1024]{2,1,0:T(8,128)S(1)}, f32[4,16,1024]{2,1,0:T(8,128)S(1)}, f32[4,16,1024]{2,1,0:T(8,128)S(1)}) fusion(f32[4,96,1024]{2,1,0:T(8,128)S(1)} %copy-done.2, f32[4,16,256]{2,1,0:T(8,128)S(1)} %fusion.58, f32[4,16,768]{2,1,0:T(8,128)} %slice_select_fusion), kind=kLoop, calls=%fused_computation.153 | loop fusion | flops 131072 | bytes 1835008 | tf_op jit(solution)/shard_map/slice | solution.py:188
  41.9 2.9 %fusion.46 = f32[4,16,1024]{2,1,0:T(8,128)S(1)} fusion(s32[1024]{0:T(1024)S(1)} %bitcast.139, f32[4,16,256]{2,1,0:T(8,128)} %collective-permute-done.4, f32[4,16,1024]{2,1,0:T(8,128)S(1)} %get-tuple-element.74, f32[4]{0:T(128)S(1)} %copy-done.35, pred[1024]{0:T(1024)(128)(4,1)S(1)} %copy-done.32, f32[4,96,1024]{2,1,0:T(8,128)S(1)} %copy-done.2), kind=kOutput, calls=%fused_computation.36 | convolution fusion | flops 1008222208 | bytes 857104 | tf_op jit(solution)/shard_map/xiz,zy->xiy/dot_general | solution.py:86
  45.1 3.1 %fusion.52 = f32[4,16,1024]{2,1,0:T(8,128)S(1)} fusion(s32[1024]{0:T(1024)S(1)} %bitcast.138, f32[4,16,256]{2,1,0:T(8,128)} %collective-permute-done.5, f32[4,16,1024]{2,1,0:T(8,128)S(1)} %get-tuple-element.72, f32[4]{0:T(128)S(1)} %copy-done.35, pred[1024]{0:T(1024)(128)(4,1)S(1)} %copy-done.31, f32[4,96,1024]{2,1,0:T(8,128)S(1)} %copy-done.2), kind=kOutput, calls=%fused_computation.38 | convolution fusion | flops 1008222208 | bytes 857104 | tf_op jit(solution)/shard_map/xiz,zy->xiy/dot_general | solution.py:86
  49.0 5.4 %collective-permute-done = f32[1,4,65536]{2,1,0:T(4,128)} collective-permute-done((f32[1,4,65536]{2,1,0:T(4,128)}, f32[1,4,65536]{2,1,0:T(4,128)}, u32[]{:S(2)}, u32[]{:S(2)}) %collective-permute-start) | collective-permute-done | bytes 1048608 | tf_op jit(solution)/shard_map/ppermute | solution.py:213
  54.4 22.7 %collective-permute-done.2 = f32[1,4,65536]{2,1,0:T(4,128)S(1)} collective-permute-done((f32[1,4,65536]{2,1,0:T(4,128)}, f32[1,4,65536]{2,1,0:T(4,128)S(1)}, u32[]{:S(2)}, u32[]{:S(2)}) %collective-permute-start.2) | collective-permute-done | bytes 1048608 | tf_op jit(solution)/shard_map/ppermute | solution.py:211
  77.2 4.0 %bitcast_add_fusion.1 = f32[4,65536]{1,0:T(4,128)S(1)} fusion(f32[4,65536]{1,0:T(4,128)S(1)} %bitcast.123, f32[1,4,65536]{2,1,0:T(4,128)S(1)} %collective-permute-done.2, f32[1,4,65536]{2,1,0:T(4,128)} %collective-permute-done.1, f32[1,4,65536]{2,1,0:T(4,128)} %collective-permute-done, f32[]{:T(128)} %bitcast.14, f32[]{:T(128)} %bitcast.12, f32[]{:T(128)} %bitcast.10), kind=kLoop, calls=%fused_computation.41 | loop fusion | flops 1572864 | bytes 5242892 | tf_op jit(solution)/shard_map/add | solution.py:222
  81.1 1.9 %fusion.24 = f32[4,64,1024]{2,1,0:T(8,128)S(1)} fusion(f32[4,96,1024]{2,1,0:T(8,128)S(1)} %fusion.78, f32[96,64,1]{0,1,2:T(8,128)S(1)} %copy-done.17, f32[1,4,64,1024]{3,1,2,0:T(4,128)S(1)} %bitcast.124, f32[4,64,1024]{2,1,0:T(8,128)S(1)} %copy-done.5, f32[1,64,1024]{2,1,0:T(8,128)S(1)} %get-tuple-element.70, f32[1,64,1024]{2,1,0:T(8,128)S(1)} %copy-done.7, ...), kind=kOutput, calls=%fused_computation.28 | convolution fusion | flops 303562752 | bytes 5791744 | tf_op jit(solution)/shard_map/bc,sbh->sch/dot_general | solution.py:171
  83.1 1.3 %fusion.57 = f32[1,4,64,1024]{3,2,1,0:T(8,128)} fusion(f32[1,4,64,1024]{3,2,1,0:T(8,128)S(1)} %copy-done, f32[4,64,1024]{2,1,0:T(8,128)S(1)} %fusion.24), kind=kLoop, calls=%fused_computation.47 | loop fusion | flops 524288 | bytes 3145728 | tf_op jit(solution)/shard_map/broadcast_in_dim | solution.py:248
  (99 shorter events, 2.4 us)
Async XLA Ops:
  0.6 8.2 %copy-start.16 = (f32[96,64,1]{0,1,2:T(8,128)S(1)}, f32[96,64,1]{0,1,2:T(8,128)}, u32[]{:S(2)}) copy-start(f32[96,64,1]{0,1,2:T(8,128)} %constant.260) | copy-start | bytes 73732
  0.6 8.2 %copy-start = (f32[1,4,64,1024]{3,2,1,0:T(8,128)S(1)}, f32[1,4,64,1024]{3,2,1,0:T(8,128)}, u32[]{:S(2)}) copy-start(f32[1,4,64,1024]{3,2,1,0:T(8,128)} %param.21) | copy-start | bytes 3145732
  3.6 14.6 %copy-start.26 = (s32[6,1024]{1,0:T(8,128)S(1)}, s32[6,1024]{1,0:T(8,128)}, u32[]{:S(2)}) copy-start(s32[6,1024]{1,0:T(8,128)} %param.25) | copy-start | bytes 73732
  3.7 15.2 %copy-start.19 = (f32[3,1024]{1,0:T(4,128)S(1)}, f32[3,1024]{1,0:T(4,128)}, u32[]{:S(2)}) copy-start(f32[3,1024]{1,0:T(4,128)} %param.22) | copy-start | bytes 36868
  3.7 16.5 %copy-start.20 = (f32[3,1024]{1,0:T(4,128)S(1)}, f32[3,1024]{1,0:T(4,128)}, u32[]{:S(2)}) copy-start(f32[3,1024]{1,0:T(4,128)} %param.23) | copy-start | bytes 36868
  3.7 16.5 %copy-start.25 = (s32[6,1024]{1,0:T(8,128)S(1)}, s32[6,1024]{1,0:T(8,128)}, u32[]{:S(2)}) copy-start(s32[6,1024]{1,0:T(8,128)} %param.24) | copy-start | bytes 73732
  3.7 44.6 %collective-permute-start.1 = (f32[1,4,65536]{2,1,0:T(4,128)}, f32[1,4,65536]{2,1,0:T(4,128)}, u32[]{:S(2)}, u32[]{:S(2)}) collective-permute-start(f32[1,4,65536]{2,1,0:T(4,128)} %reshape_squeeze.3), channel_id=1, source_target_pairs={{0,8},{8,16},{16,24},{24,0},{1,9},{9,17},{17,25},{25,1},{2,10},{10... | collective-permute-start | bytes 3145736 | tf_op jit(solution)/shard_map/ppermute | solution.py:211
  6.8 47.6 %collective-permute-start = (f32[1,4,65536]{2,1,0:T(4,128)}, f32[1,4,65536]{2,1,0:T(4,128)}, u32[]{:S(2)}, u32[]{:S(2)}) collective-permute-start(f32[1,4,65536]{2,1,0:T(4,128)} %reshape_squeeze.3), channel_id=1, source_target_pairs={{0,24},{8,0},{16,8},{24,16},{1,25},{9,1},{17,9},{25,17},{2,26},{10... | collective-permute-start | bytes 3145736 | tf_op jit(solution)/shard_map/ppermute | solution.py:213
  10.3 18.3 %copy-start.1 = (f32[4,96,1024]{2,1,0:T(8,128)}, f32[4,96,1024]{2,1,0:T(8,128)S(1)}, u32[]{:S(2)}) copy-start(f32[4,96,1024]{2,1,0:T(8,128)S(1)} %convolution_bitcast_fusion) | copy-start | bytes 4718596
  10.3 11.8 %copy-start.36 = (f32[4]{0:T(128)S(1)}, f32[4]{0:T(128)}, u32[]{:S(2)}) copy-start(f32[4]{0:T(128)} %constant.251.clone.1) | copy-start | bytes 52
  11.0 33.8 %collective-permute-start.5 = (f32[4,16,256]{2,1,0:T(8,128)}, f32[4,16,256]{2,1,0:T(8,128)}, u32[]{:S(2)}, u32[]{:S(2)}) collective-permute-start(f32[4,16,256]{2,1,0:T(8,128)} %get-tuple-element.75), channel_id=1, source_target_pairs={{1,0},{3,2},{5,4},{7,6},{9,8},{11,10},{13,12},{15,14},{17,16},{19,... | collective-permute-start | bytes 196616 | tf_op jit(solution)/shard_map/ppermute | solution.py:23
  12.3 29.5 %collective-permute-start.4 = (f32[4,16,256]{2,1,0:T(8,128)}, f32[4,16,256]{2,1,0:T(8,128)}, u32[]{:S(2)}, u32[]{:S(2)}) collective-permute-start(f32[4,16,256]{2,1,0:T(8,128)} %get-tuple-element.76), channel_id=1, source_target_pairs={{0,1},{2,3},{4,5},{6,7},{8,9},{10,11},{12,13},{14,15},{16,17},{18,... | collective-permute-start | bytes 196616 | tf_op jit(solution)/shard_map/ppermute | solution.py:22
  18.1 21.4 %collective-permute-start.3 = (f32[4,16,256]{2,1,0:T(8,128)}, f32[4,16,256]{2,1,0:T(8,128)}, u32[]{:S(2)}, u32[]{:S(2)}) collective-permute-start(f32[4,16,256]{2,1,0:T(8,128)} %get-tuple-element.77), channel_id=1, source_target_pairs={{0,6},{2,0},{4,2},{6,4},{1,7},{3,1},{5,3},{7,5},{8,14},{10,8},{12,... | collective-permute-start | bytes 196616 | tf_op jit(solution)/shard_map/ppermute | solution.py:30
  18.9 4.9 %copy-start.21 = (f32[1,1024]{1,0:T(1,128)}, f32[1,1024]{1,0:T(1,128)S(1)}, u32[]{:S(2)}) copy-start(f32[1,1024]{1,0:T(1,128)S(1)} %get-tuple-element.101) | copy-start | bytes 12292
  18.9 4.9 %copy-start.23 = (f32[1,1024]{1,0:T(1,128)}, f32[1,1024]{1,0:T(1,128)S(1)}, u32[]{:S(2)}) copy-start(f32[1,1024]{1,0:T(1,128)S(1)} %get-tuple-element.100) | copy-start | bytes 12292
  26.9 3.4 %copy-start.18 = (f32[3,64,64,1]{2,1,3,0:T(8,128)S(1)}, f32[3,64,64,1]{2,1,3,0:T(8,128)}, u32[]{:S(2)}) copy-start(f32[3,64,64,1]{2,1,3,0:T(8,128)} %constant.259) | copy-start | bytes 147460
  36.6 4.3 %copy-start.2 = (f32[4,96,1024]{2,1,0:T(8,128)S(1)}, f32[4,96,1024]{2,1,0:T(8,128)}, u32[]{:S(2)}) copy-start(f32[4,96,1024]{2,1,0:T(8,128)} %copy-done.1) | copy-start | bytes 4718596
  44.8 3.5 %copy-start.6 = (f32[4,96,1024]{2,1,0:T(8,128)S(1)}, f32[4,96,1024]{2,1,0:T(8,128)}, u32[]{:S(2)}) copy-start(f32[4,96,1024]{2,1,0:T(8,128)} %fusion.92) | copy-start | bytes 4718596
  44.8 3.5 %copy-start.24 = (f32[1,1024]{1,0:T(1,128)S(1)}, f32[1,1024]{1,0:T(1,128)}, u32[]{:S(2)}) copy-start(f32[1,1024]{1,0:T(1,128)} %copy-done.23) | copy-start | bytes 12292
  45.1 3.4 %copy-start.11 = (f32[4,16,1024]{2,1,0:T(8,128)S(1)}, f32[4,16,1024]{2,1,0:T(8,128)}, u32[]{:S(2)}) copy-start(f32[4,16,1024]{2,1,0:T(8,128)} %copy-done.10) | copy-start | bytes 786436
  45.1 3.4 %copy-start.14 = (f32[1,16,1024]{2,1,0:T(8,128)S(1)}, f32[1,16,1024]{2,1,0:T(8,128)}, u32[]{:S(2)}) copy-start(f32[1,16,1024]{2,1,0:T(8,128)} %get-tuple-element.84) | copy-start | bytes 196612
  45.1 3.4 %copy-start.15 = (f32[1,16,1024]{2,1,0:T(8,128)S(1)}, f32[1,16,1024]{2,1,0:T(8,128)}, u32[]{:S(2)}) copy-start(f32[1,16,1024]{2,1,0:T(8,128)} %get-tuple-element.85) | copy-start | bytes 196612
  45.1 3.4 %copy-start.28 = (f32[1024]{0:T(1024)S(1)}, f32[1024]{0:T(1024)}, u32[]{:S(2)}) copy-start(f32[1024]{0:T(1024)} %broadcast_multiply_fusion.1) | copy-start | bytes 12292
  45.1 3.4 %copy-start.9 = (f32[4,16,1024]{2,1,0:T(8,128)S(1)}, f32[4,16,1024]{2,1,0:T(8,128)}, u32[]{:S(2)}) copy-start(f32[4,16,1024]{2,1,0:T(8,128)} %copy-done.8) | copy-start | bytes 786436
  45.1 3.4 %copy-start.12 = (f32[1,16,1024]{2,1,0:T(8,128)S(1)}, f32[1,16,1024]{2,1,0:T(8,128)}, u32[]{:S(2)}) copy-start(f32[1,16,1024]{2,1,0:T(8,128)} %get-tuple-element.82) | copy-start | bytes 196612
  45.1 3.4 %copy-start.13 = (f32[1,16,1024]{2,1,0:T(8,128)S(1)}, f32[1,16,1024]{2,1,0:T(8,128)}, u32[]{:S(2)}) copy-start(f32[1,16,1024]{2,1,0:T(8,128)} %get-tuple-element.83) | copy-start | bytes 196612
  45.1 3.4 %copy-start.22 = (f32[1,1024]{1,0:T(1,128)S(1)}, f32[1,1024]{1,0:T(1,128)}, u32[]{:S(2)}) copy-start(f32[1,1024]{1,0:T(1,128)} %copy-done.21) | copy-start | bytes 12292
  48.3 28.8 %collective-permute-start.2 = (f32[1,4,65536]{2,1,0:T(4,128)}, f32[1,4,65536]{2,1,0:T(4,128)S(1)}, u32[]{:S(2)}, u32[]{:S(2)}) collective-permute-start(f32[1,4,65536]{2,1,0:T(4,128)} %collective-permute-done.1), channel_id=1, source_target_pairs={{0,8},{8,16},{16,24},{24,0},{1,9},{9,17},{17,25},{25,1},{2,10},{10... | collective-permute-start | bytes 3145736 | tf_op jit(solution)/shard_map/ppermute | solution.py:211
  48.4 28.7 %copy-start.4 = (f32[1,4,64,1024]{3,1,2,0:T(4,128)S(1)}, f32[1,4,64,1024]{3,1,2,0:T(4,128)}, u32[]{:S(2)}) copy-start(f32[1,4,64,1024]{3,1,2,0:T(4,128)} %copy.12) | copy-start | bytes 3145732
  77.1 4.0 %copy-start.5 = (f32[4,64,1024]{2,1,0:T(8,128)S(1)}, f32[4,64,1024]{2,1,0:T(8,128)}, u32[]{:S(2)}) copy-start(f32[4,64,1024]{2,1,0:T(8,128)} %get-tuple-element.106) | copy-start | bytes 3145732
  77.2 4.0 %copy-start.7 = (f32[1,64,1024]{2,1,0:T(8,128)S(1)}, f32[1,64,1024]{2,1,0:T(8,128)}, u32[]{:S(2)}) copy-start(f32[1,64,1024]{2,1,0:T(8,128)} %get-tuple-element.71) | copy-start | bytes 786436
  77.2 4.0 %copy-start.17 = (f32[96,64,1]{0,1,2:T(8,128)S(1)}, f32[96,64,1]{0,1,2:T(8,128)}, u32[]{:S(2)}) copy-start(f32[96,64,1]{0,1,2:T(8,128)} %constant.260) | copy-start | bytes 73732
  (12 other events, 25.4 us)
